TPU v7x, 32 devices: a whole 2x2x4 slice. The times are simulated.
32 devices in a mesh: gx: 4 (over y, x), gy: 8 (over z, core).
Axes of the slice: x: 2, y: 2, z: 4, core: 2. Of those that a mesh axis runs over, the one named last changes fastest.
Arguments:
- posterior: bfloat16 [8192, 1000], P(('gx', 'gy')), may hold values from -6 to 6
- class_affinity: bfloat16 [8192, 1000], P(('gx', 'gy')), may hold values from 0.049804688 to 20
- band_tiles: bfloat16 [64, 4, 128, 128], P(('gx', 'gy')), may hold values from 9.9658966e-05 to 1
- band_offset: int32 [64, 4], P(('gx', 'gy')), may hold values from -1 to 1
- band_count: int32 [64], P(('gx', 'gy')), may hold values from 1 to 4
- far_tiles: bfloat16 [32, 4, 128, 128], P(('gx', 'gy')), may hold values from 9.9658966e-05 to 1
- far_row: int32 [32, 4], P(('gx', 'gy')), may hold values from 0 to 1
- far_block: int32 [32, 4], P(('gx', 'gy')), may hold values from 0 to 1
Outputs:
- propagated: bfloat16 [8192, 1000], P(('gx', 'gy'))
Inputs may be any that keep to these rules, and one draw needn't show every extreme that they name: Near tiles of a slot index at or above band_count of their row block are not part of the graph.
All inputs are finite; a program needn't handle non-finite values.
Results may differ from a plain program's by a relative error of at most 0.002.
Values may be sent and summed in bfloat16 or wider, within the bound.
A program may use at most 64 MiB of HBM per device.

v0:
```python
import jax
import jax.numpy as jnp
from jax import lax
from jax.sharding import PartitionSpec as P

BAND_REACH = 1
SWEEPS = 2


propagation_weight = 0.9
epsilon = 1e-06


def padded(value, sides, width):
    for axis, dim in sides:
        peers, length = (lax.axis_size(axis), value.shape[dim])
        up = [(i, (i + 1) % peers) for i in range(peers)]
        down = [(j, i) for i, j in up]
        last = lax.slice_in_dim(value, length - width, length, axis=dim)
        initial = lax.slice_in_dim(value, 0, width, axis=dim)
        before = lax.ppermute(last, axis, up)
        after = lax.ppermute(initial, axis, down)
        value = jnp.concatenate([before, value, after], axis=dim)
    return value


def normalize(mixed_rows):
    row_scale = lax.rsqrt(jnp.mean(mixed_rows * mixed_rows, axis=-1, keepdims=True) + epsilon)
    return (mixed_rows * row_scale).astype(jnp.bfloat16)


def local(
    posterior, class_affinity, band_tiles, band_offset, band_count, far_tiles, far_row, far_block
):
    row_count, class_count = posterior.shape
    tile_size = band_tiles.shape[-1]
    block_count = row_count // tile_size
    slot_count = band_tiles.shape[1]
    peer_count = lax.axis_size("gx")
    wanted = lax.all_to_all(
        far_block.reshape(peer_count), "gx", split_axis=0, concat_axis=0, tiled=True
    )
    slot_ids = jnp.arange(slot_count, dtype=jnp.int32)
    block_ids = jnp.arange(block_count, dtype=jnp.int32)
    is_live = slot_ids[None, :] < band_count[:, None]
    owner_table = (far_row.reshape(peer_count)[None, :] == block_ids[:, None]).astype(jnp.bfloat16)
    far_weights = far_tiles.reshape(peer_count, tile_size, tile_size)
    far_matrix = (
        owner_table[:, None, :, None] * jnp.transpose(far_weights, (1, 0, 2))[None]
    ).reshape(row_count, peer_count * tile_size)
    rim_depth = BAND_REACH
    source_index = block_ids[:, None] + rim_depth + band_offset
    masked_tiles = band_tiles * is_live.astype(jnp.bfloat16)[:, :, None, None]
    current = posterior
    for sweep in range(SWEEPS):
        extended = padded(current, (("gy", 0),), rim_depth * tile_size)
        outgoing = current.reshape(block_count, tile_size, class_count)[wanted].reshape(
            peer_count * tile_size, class_count
        )
        arrived = lax.all_to_all(outgoing, "gx", split_axis=0, concat_axis=0, tiled=True)
        ext_blocks = extended.reshape(-1, tile_size, class_count)
        gathered = ext_blocks[source_index]
        band_sum = jnp.einsum(
            "bsij,bsjc->bic", masked_tiles, gathered, preferred_element_type=jnp.float32
        ).reshape(row_count, class_count)
        far_sum = jnp.dot(far_matrix, arrived, preferred_element_type=jnp.float32)
        mixed_rows = propagation_weight * (band_sum + far_sum) + class_affinity.astype(jnp.float32)
        current = normalize(mixed_rows)
    return current


def solution(mesh):
    in_specs = (
        P(("gx", "gy"), None),
        P(("gx", "gy"), None),
        P(("gx", "gy"), None, None, None),
        P(("gx", "gy"), None),
        P(("gx", "gy")),
        P(("gx", "gy"), None, None, None),
        P(("gx", "gy"), None),
        P(("gx", "gy"), None),
    )
    out_specs = P(("gx", "gy"), None)
    return jax.shard_map(local, mesh=mesh, in_specs=in_specs, out_specs=out_specs, check_vma=False)
```

profile of v0, /device:TPU:0, one launch (start us, length us, event | category | flops | bytes accessed | tf_op | source)
XLA Modules:
  0.0 56.3 jit_solution(4133630194379111473)
XLA Ops:
  0.0 1.1 %fusion.15 = (bf16[128,1000]{0,1:T(8,128)(2,1)S(1)}, bf16[128,1000]{0,1:T(8,128)(2,1)S(1)}) fusion(bf16[256,1000]{0,1:T(8,128)(2,1)} %param.8), kind=kLoop, calls=%fused_computation.40 | loop fusion | bytes 1024000 | tf_op jit(solution)/shard_map/slice | solution.py:19
  1.7 4.1 %collective-permute-start.1 = (bf16[128,1000]{0,1:T(8,128)(2,1)S(1)}, bf16[128,1000]{0,1:T(8,128)(2,1)S(1)}, u32[]{:S(2)}, u32[]{:S(2)}) collective-permute-start(bf16[128,1000]{0,1:T(8,128)(2,1)S(1)} %get-tuple-element.8), channel_id=1, source_target_pairs={{1,0},{2,1},{3,2},{4,3},{5,4},{6,5},{7,6},{0,7},{9,8},{10,9},{11,1... | collective-permute-start | bytes 768008 | tf_op jit(solution)/shard_map/ppermute | solution.py:22
  5.8 1.3 %copy.49 = s32[4,1,1]{2,1,0:T(1,128)} copy(s32[4,1,1]{0,2,1:T(1,128)} %bitcast.59) | data formatting | bytes 32 | tf_op jit(solution)/shard_map/all_to_all | solution.py:40
  7.1 4.2 %all-to-all-start = ((s32[4,1,1]{2,1,0:T(1,128)}), s32[4,1,1]{2,1,0:T(1,128)S(1)}, u32[]{:S(2)}, u32[]{:S(2)}) async-start(s32[4,1,1]{2,1,0:T(1,128)} %copy.49), calls=%async_computation | async-start | bytes 4096 | tf_op jit(solution)/shard_map/all_to_all | solution.py:40
  11.3 1.2 %copy.48 = bf16[256,1000]{1,0:T(8,128)(2,1)S(1)} copy(bf16[256,1000]{0,1:T(8,128)(2,1)} %param.8) | data formatting | bytes 1024000 | tf_op args[0]
  13.1 2.8 %all-to-all-done = s32[4,1,1]{2,1,0:T(1,128)S(1)} async-done(((s32[4,1,1]{2,1,0:T(1,128)}), s32[4,1,1]{2,1,0:T(1,128)S(1)}, u32[]{:S(2)}, u32[]{:S(2)}) %all-to-all-start) | async-done | bytes 48 | tf_op jit(solution)/shard_map/all_to_all | solution.py:40
  16.1 1.6 %gather_fusion.1 = bf16[4,128,1000]{1,2,0:T(8,128)(2,1)} fusion(bf16[2,128,1000]{1,2,0:T(8,128)(2,1)S(1)} %copy.50, s32[1024]{0:T(1024)S(1)} %pad_clamp_fusion), kind=kCustom, calls=%fused_computation.1 | custom fusion | bytes 2048016 | tf_op jit(solution)/shard_map/gather | solution.py:57
  17.7 4.2 %all-to-all-start.1 = ((bf16[4,128,1000]{1,2,0:T(8,128)(2,1)}), bf16[4,128,1000]{1,2,0:T(8,128)(2,1)}, u32[]{:S(2)}, u32[]{:S(2)}) async-start(bf16[4,128,1000]{1,2,0:T(8,128)(2,1)} %gather_fusion.1), calls=%async_computation.1 | async-start | bytes 2048000 | tf_op jit(solution)/shard_map/all_to_all | solution.py:60
  23.0 0.6 %copy.45 = bf16[4,128,1000]{1,2,0:T(8,128)(2,1)S(1)} copy(bf16[4,128,1000]{2,1,0:T(8,128)(2,1)S(1)} %bitcast.53) | data formatting | bytes 2048000 | tf_op jit(solution)/shard_map/reshape | solution.py:61
  23.6 0.9 %gather_fusion = bf16[8,128,1000]{1,2,0:T(8,128)(2,1)S(1)} fusion(bf16[4,128,1000]{1,2,0:T(8,128)(2,1)S(1)} %copy.45, s32[1024]{0:T(1024)S(1)} %pad_clamp_fusion.1), kind=kCustom, calls=%fused_computation | custom fusion | bytes 4096032 | tf_op jit(solution)/shard_map/gather | solution.py:62
  24.6 1.7 %fusion.9 = f32[2,128,1000,1]{2,1,3,0:T(8,128)S(1)} fusion(bf16[2,4,128,1000]{2,3,1,0:T(8,128)(2,1)S(1)} %bitcast.50, bf16[2,4,128,128]{3,2,1,0:T(8,128)(2,1)} %param.10, bf16[2,4]{1,0:T(2,128)(2,1)S(1)} %compare_convert_fusion.1), kind=kOutput, calls=%fused_computation.24 | convolution fusion | flops 262275072 | bytes 3334160 | tf_op jit(solution)/shard_map/bsij,bsjc->bic/dot_general | solution.py:63
  26.3 1.3 %copy.52 = f32[256,1000]{0,1:T(8,128)} copy(f32[256,1000]{1,0:T(8,128)S(1)} %bitcast.54) | data formatting | bytes 2048000 | tf_op jit(solution)/shard_map/reshape | solution.py:65
  27.6 5.0 %all-to-all-done.1 = bf16[4,128,1000]{1,2,0:T(8,128)(2,1)} async-done(((bf16[4,128,1000]{1,2,0:T(8,128)(2,1)}), bf16[4,128,1000]{1,2,0:T(8,128)(2,1)}, u32[]{:S(2)}, u32[]{:S(2)}) %all-to-all-start.1) | async-done | bytes 1024032 | tf_op jit(solution)/shard_map/all_to_all | solution.py:60
  32.6 1.5 %copy.51 = bf16[4,128,1000]{2,1,0:T(8,128)(2,1)S(1)} copy(bf16[4,128,1000]{1,2,0:T(8,128)(2,1)} %all-to-all-done.1) | data formatting | bytes 2048000 | tf_op jit(solution)/shard_map/all_to_all | solution.py:60
  34.2 0.6 %multiply_reduce_fusion.1 = (f32[256]{0:T(256)S(1)}, f32[256,1000]{0,1:T(8,128)S(1)}) fusion(bf16[256,1000]{0,1:T(8,128)(2,1)S(1)} %copy-done.2, f32[256,1000]{0,1:T(8,128)S(1)} %copy-done.1, bf16[512,1000]{1,0:T(8,128)(2,1)S(1)} %bitcast.52, bf16[32,8,4,128]{3,2,1,0:T(4,128)(2,1)S(1)} %bitcast.55), kind=kOutput, calls=%fused_computation.17 | convolution fusion | flops 263679744 | bytes 3847168 | tf_op jit(solution)/shard_map/dot_general | solution.py:66
  35.0 1.7 %gather_fusion.3 = bf16[4,128,1000]{1,2,0:T(8,128)(2,1)} fusion(bf16[2,128,1000]{1,2,0:T(8,128)(2,1)S(1)} %copy_bitcast_fusion.1, s32[1024]{0:T(1024)S(1)} %pad_clamp_fusion), kind=kCustom, calls=%fused_computation.3 | custom fusion | bytes 2048016 | tf_op jit(solution)/shard_map/gather | solution.py:57
  36.6 4.2 %all-to-all-start.2 = ((bf16[4,128,1000]{1,2,0:T(8,128)(2,1)}), bf16[4,128,1000]{1,2,0:T(8,128)(2,1)}, u32[]{:S(2)}, u32[]{:S(2)}) async-start(bf16[4,128,1000]{1,2,0:T(8,128)(2,1)} %gather_fusion.3), calls=%async_computation.2 | async-start | bytes 2048000 | tf_op jit(solution)/shard_map/all_to_all | solution.py:60
  41.0 3.5 %collective-permute-start.3 = (bf16[128,1000]{0,1:T(8,128)(2,1)S(1)}, bf16[128,1000]{0,1:T(8,128)(2,1)S(1)}, u32[]{:S(2)}, u32[]{:S(2)}) collective-permute-start(bf16[128,1000]{0,1:T(8,128)(2,1)S(1)} %get-tuple-element.6), channel_id=1, source_target_pairs={{1,0},{2,1},{3,2},{4,3},{5,4},{6,5},{7,6},{0,7},{9,8},{10,9},{11,1... | collective-permute-start | bytes 768008 | tf_op jit(solution)/shard_map/ppermute | solution.py:22
  44.5 5.8 %collective-permute-done.2 = bf16[128,1000]{0,1:T(8,128)(2,1)S(1)} collective-permute-done((bf16[128,1000]{0,1:T(8,128)(2,1)S(1)}, bf16[128,1000]{0,1:T(8,128)(2,1)S(1)}, u32[]{:S(2)}, u32[]{:S(2)}) %collective-permute-start.2) | collective-permute-done | bytes 256032 | tf_op jit(solution)/shard_map/ppermute | solution.py:21
  50.4 0.9 %gather_fusion.2 = bf16[8,128,1000]{1,2,0:T(8,128)(2,1)S(1)} fusion(bf16[4,128,1000]{1,2,0:T(8,128)(2,1)S(1)} %copy_bitcast_fusion, s32[1024]{0:T(1024)S(1)} %pad_clamp_fusion.1), kind=kCustom, calls=%fused_computation.2 | custom fusion | bytes 4096032 | tf_op jit(solution)/shard_map/gather | solution.py:62
  51.4 1.7 %convolution_bitcast_fusion = f32[2,125,8,128]{3,2,1,0:T(8,128)S(1)} fusion(bf16[2,4,128,1000]{2,3,1,0:T(8,128)(2,1)S(1)} %bitcast.49, bf16[2,4,128,128]{3,2,1,0:T(8,128)(2,1)} %param.10, bf16[2,4]{1,0:T(2,128)(2,1)S(1)} %compare_convert_fusion.1), kind=kOutput, calls=%fused_computation.7 | convolution fusion | flops 262275072 | bytes 3334160 | tf_op jit(solution)/shard_map/bsij,bsjc->bic/dot_general | solution.py:63
  53.3 1.5 %copy.56 = bf16[4,128,1000]{2,1,0:T(8,128)(2,1)S(1)} copy(bf16[4,128,1000]{1,2,0:T(8,128)(2,1)} %all-to-all-done.2) | data formatting | bytes 2048000 | tf_op jit(solution)/shard_map/all_to_all | solution.py:60
  54.8 0.6 %multiply_reduce_fusion = (f32[256]{0:T(256)S(1)}, f32[256,1000]{0,1:T(8,128)S(1)}) fusion(bf16[256,1000]{0,1:T(8,128)(2,1)S(1)} %copy-done.3, bf16[512,1000]{1,0:T(8,128)(2,1)S(1)} %bitcast.51, bf16[32,8,4,128]{3,2,1,0:T(4,128)(2,1)S(1)} %bitcast.56, f32[2,125,8,128]{3,2,1,0:T(8,128)S(1)} %convolution_bitcast_fusion), kind=kOutput, calls=%fused_computation.15 | convolution fusion | flops 263679744 | bytes 3847168 | tf_op jit(solution)/shard_map/dot_general | solution.py:66
  55.4 0.9 %multiply_convert_fusion = bf16[256,1000]{0,1:T(8,128)(2,1)} fusion(f32[256,1000]{0,1:T(8,128)S(1)} %get-tuple-element.12, f32[256]{0:T(256)S(1)} %add_rsqrt_fusion), kind=kLoop, calls=%fused_computation.14 | loop fusion | flops 512000 | bytes 1537024 | tf_op jit(solution)/shard_map/convert_element_type | solution.py:29
  (42 shorter events, 2.8 us)
Async XLA Ops:
  0.0 12.5 %copy-start.5 = (s32[2,4]{1,0:T(2,128)S(1)}, s32[2,4]{1,0:T(2,128)}, u32[]{:S(2)}) copy-start(s32[2,4]{1,0:T(2,128)} %param.11) | copy-start | bytes 100
  0.0 12.7 %copy-start.6 = (s32[2]{0:T(128)S(1)}, s32[2]{0:T(128)}, u32[]{:S(2)}) copy-start(s32[2]{0:T(128)} %param.12) | copy-start | bytes 28
  0.0 13.1 %copy-start.7 = (s32[1,4]{1,0:T(1,128)S(1)}, s32[1,4]{1,0:T(1,128)}, u32[]{:S(2)}) copy-start(s32[1,4]{1,0:T(1,128)} %param.14) | copy-start | bytes 52
  1.2 21.1 %collective-permute-start = (bf16[128,1000]{0,1:T(8,128)(2,1)S(1)}, bf16[128,1000]{0,1:T(8,128)(2,1)S(1)}, u32[]{:S(2)}, u32[]{:S(2)}) collective-permute-start(bf16[128,1000]{0,1:T(8,128)(2,1)S(1)} %get-tuple-element.7), channel_id=1, source_target_pairs={{0,1},{1,2},{2,3},{3,4},{4,5},{5,6},{6,7},{7,0},{8,9},{9,10},{10,1... | collective-permute-start | bytes 768008 | tf_op jit(solution)/shard_map/ppermute | solution.py:21
  1.7 20.6 %collective-permute-start.1 = (bf16[128,1000]{0,1:T(8,128)(2,1)S(1)}, bf16[128,1000]{0,1:T(8,128)(2,1)S(1)}, u32[]{:S(2)}, u32[]{:S(2)}) collective-permute-start(bf16[128,1000]{0,1:T(8,128)(2,1)S(1)} %get-tuple-element.8), channel_id=1, source_target_pairs={{1,0},{2,1},{3,2},{4,3},{5,4},{6,5},{7,6},{0,7},{9,8},{10,9},{11,1... | collective-permute-start | bytes 768008 | tf_op jit(solution)/shard_map/ppermute | solution.py:22
  7.1 8.8 %all-to-all-start = ((s32[4,1,1]{2,1,0:T(1,128)}), s32[4,1,1]{2,1,0:T(1,128)S(1)}, u32[]{:S(2)}, u32[]{:S(2)}) async-start(s32[4,1,1]{2,1,0:T(1,128)} %copy.49), calls=%async_computation | async-start | bytes 4096 | tf_op jit(solution)/shard_map/all_to_all | solution.py:40
  16.0 5.9 %copy-start.4 = (bf16[1,4,128,128]{3,2,1,0:T(8,128)(2,1)S(1)}, bf16[1,4,128,128]{3,2,1,0:T(8,128)(2,1)}, u32[]{:S(2)}) copy-start(bf16[1,4,128,128]{3,2,1,0:T(8,128)(2,1)} %param.13) | copy-start | bytes 393220
  16.1 6.2 %copy-start = (bf16[256,1000]{0,1:T(8,128)(2,1)S(1)}, bf16[256,1000]{0,1:T(8,128)(2,1)}, u32[]{:S(2)}) copy-start(bf16[256,1000]{0,1:T(8,128)(2,1)} %param.8) | copy-start | bytes 1536004
  17.7 14.9 %all-to-all-start.1 = ((bf16[4,128,1000]{1,2,0:T(8,128)(2,1)}), bf16[4,128,1000]{1,2,0:T(8,128)(2,1)}, u32[]{:S(2)}, u32[]{:S(2)}) async-start(bf16[4,128,1000]{1,2,0:T(8,128)(2,1)} %gather_fusion.1), calls=%async_computation.1 | async-start | bytes 2048000 | tf_op jit(solution)/shard_map/all_to_all | solution.py:60
  27.6 6.5 %copy-start.1 = (f32[256,1000]{0,1:T(8,128)S(1)}, f32[256,1000]{0,1:T(8,128)}, u32[]{:S(2)}) copy-start(f32[256,1000]{0,1:T(8,128)} %copy.52) | copy-start | bytes 3072004
  27.6 6.5 %copy-start.2 = (bf16[256,1000]{0,1:T(8,128)(2,1)S(1)}, bf16[256,1000]{0,1:T(8,128)(2,1)}, u32[]{:S(2)}) copy-start(bf16[256,1000]{0,1:T(8,128)(2,1)} %param.9) | copy-start | bytes 1536004
  36.6 16.6 %all-to-all-start.2 = ((bf16[4,128,1000]{1,2,0:T(8,128)(2,1)}), bf16[4,128,1000]{1,2,0:T(8,128)(2,1)}, u32[]{:S(2)}, u32[]{:S(2)}) async-start(bf16[4,128,1000]{1,2,0:T(8,128)(2,1)} %gather_fusion.3), calls=%async_computation.2 | async-start | bytes 2048000 | tf_op jit(solution)/shard_map/all_to_all | solution.py:60
  40.9 9.4 %collective-permute-start.2 = (bf16[128,1000]{0,1:T(8,128)(2,1)S(1)}, bf16[128,1000]{0,1:T(8,128)(2,1)S(1)}, u32[]{:S(2)}, u32[]{:S(2)}) collective-permute-start(bf16[128,1000]{0,1:T(8,128)(2,1)S(1)} %get-tuple-element.5), channel_id=1, source_target_pairs={{0,1},{1,2},{2,3},{3,4},{4,5},{5,6},{6,7},{7,0},{8,9},{9,10},{10,1... | collective-permute-start | bytes 768008 | tf_op jit(solution)/shard_map/ppermute | solution.py:21
  41.0 9.3 %collective-permute-start.3 = (bf16[128,1000]{0,1:T(8,128)(2,1)S(1)}, bf16[128,1000]{0,1:T(8,128)(2,1)S(1)}, u32[]{:S(2)}, u32[]{:S(2)}) collective-permute-start(bf16[128,1000]{0,1:T(8,128)(2,1)S(1)} %get-tuple-element.6), channel_id=1, source_target_pairs={{1,0},{2,1},{3,2},{4,3},{5,4},{6,5},{7,6},{0,7},{9,8},{10,9},{11,1... | collective-permute-start | bytes 768008 | tf_op jit(solution)/shard_map/ppermute | solution.py:22
  53.1 1.7 %copy-start.3 = (bf16[256,1000]{0,1:T(8,128)(2,1)S(1)}, bf16[256,1000]{0,1:T(8,128)(2,1)}, u32[]{:S(2)}) copy-start(bf16[256,1000]{0,1:T(8,128)(2,1)} %param.9) | copy-start | bytes 1536004
where the time goes:
time: 57.3 us; the launch traced here: 56.3 us
  starting transfers between devices  20.8 us (36%)
  local copies, waits for them, and re-layouts  15.1 us (26%)
  waiting for transfers between devices  13.7 us (24%)
  matrix products  4.58 us (8%)
  other arithmetic  1.81 us (3%)
    all_to_all x2, starting transfers between devices, local(): lax.all_to_all(outgoing, 'gx', split_axis=0, concat_axis=0, tiled=True)  8.47 us
    ppermute x2, starting transfers between devices, padded(): after = lax.ppermute(initial, axis, down)  7.62 us
    ppermute x2, waiting for transfers between devices, padded(): before = lax.ppermute(last, axis, up)  5.79 us
    all_to_all x2, waiting for transfers between devices, local(): lax.all_to_all(outgoing, 'gx', split_axis=0, concat_axis=0, tiled=True)  5.12 us
    all_to_all x1, starting transfers between devices, local(): lax.all_to_all(far_block.reshape(peer_count), 'gx', split_axis=0, concat_...  4.15 us
    dot_general x2, matrix products, local(): jnp.einsum('bsij,bsjc->bic', masked_tiles, gathered, preferred_element_ty...  3.44 us
    gather x2, local copies, waits for them, and re-layouts, local(): current.reshape(block_count, tile_size, class_count)[wanted]  3.32 us
    all_to_all x2, local copies, waits for them, and re-layouts, local(): lax.all_to_all(outgoing, 'gx', split_axis=0, concat_axis=0, tiled=True)  3.07 us
  transfers between devices with their start and end apart: 7, of which 4 were waited for; matrix products, arithmetic and copies ran while one was open for 24% of the time, Pallas kernels for 0%

commit v1 on v0

v1 whole, which is shorter than its diff:
```python
import functools

import jax
import jax.numpy as jnp
from jax import lax
from jax.experimental import pallas as pl
from jax.experimental.pallas import tpu as pltpu
from jax.sharding import PartitionSpec as P

SWEEPS = 2
propagation_weight = 0.9
epsilon = 1e-06
MESH = pl.DeviceIdType.MESH


def partner(me, step, peers):
    total = 0
    bit = 1
    while bit < peers:
        here = lax.rem(me // bit, 2)
        total = total + bit * (lax.rem(here + 1, 2) if step & bit else here)
        bit *= 2
    return total


def kernel(
    peers, ring,
    post, aff_hbm, band_hbm, far_hbm, boff, bcnt, frow, fblk,
    out,
    own, exts, stage, arrived, ask, asked, aff, band, far, near_weights, far_weights, acc,
    load_sem, halo_send, halo_recv, far_send, far_recv, ask_send, ask_recv,
):
    me = lax.axis_index("gx")
    spot = lax.axis_index("gy")
    up = lax.rem(spot + 1, ring)
    down = lax.rem(spot + ring - 1, ring)
    blocks, slots, tile, _ = band.shape
    classes = post.shape[0]
    steps = sorted(range(1, peers), key=lambda r: (-bin(r).count("1"), r))
    mates = {r: partner(me, r, peers) for r in range(peers)}

    barrier = pltpu.get_barrier_semaphore()
    for r in steps:
        pl.semaphore_signal(barrier, inc=1, device_id={"gx": mates[r]}, device_id_type=MESH)
    for side in (up, down):
        pl.semaphore_signal(barrier, inc=1, device_id={"gy": side}, device_id_type=MESH)

    def block_of(ref, b):
        return ref.at[:, pl.ds(b * tile, tile)]

    loads = [
        pltpu.make_async_copy(block_of(post, b), target, load_sem.at[3 + 2 * b + k])
        for b in range(blocks)
        for k, target in enumerate((own[0].at[b], exts[0].at[1 + b]))
    ]
    band_load = pltpu.make_async_copy(band_hbm, band, load_sem.at[0])
    far_load = pltpu.make_async_copy(far_hbm, far, load_sem.at[1])
    aff_load = pltpu.make_async_copy(aff_hbm, aff, load_sem.at[2])
    for load in loads + [band_load, far_load, aff_load]:
        load.start()
    for r in steps:
        ask[r] = jnp.full(ask.shape[1:], fblk[0, mates[r]], jnp.int32)
    pl.semaphore_wait(barrier, len(steps) + 2)

    def question(r):
        return pltpu.make_async_remote_copy(
            src_ref=ask.at[r], dst_ref=asked.at[r],
            send_sem=ask_send.at[r], recv_sem=ask_recv.at[r],
            device_id={"gx": mates[r]}, device_id_type=MESH,
        )

    def far_copy(sweep, r):
        return pltpu.make_async_remote_copy(
            src_ref=stage.at[sweep, r], dst_ref=arrived.at[sweep, r],
            send_sem=far_send.at[sweep, r], recv_sem=far_recv.at[sweep, r],
            device_id={"gx": mates[r]}, device_id_type=MESH,
        )

    def halo_copies(sweep, source):
        return [
            pltpu.make_async_remote_copy(
                src_ref=source(blocks - 1), dst_ref=exts[sweep].at[0],
                send_sem=halo_send.at[sweep, 0], recv_sem=halo_recv.at[sweep, 0],
                device_id={"gy": up}, device_id_type=MESH,
            ),
            pltpu.make_async_remote_copy(
                src_ref=source(0), dst_ref=exts[sweep].at[blocks + 1],
                send_sem=halo_send.at[sweep, 1], recv_sem=halo_recv.at[sweep, 1],
                device_id={"gy": down}, device_id_type=MESH,
            ),
        ]

    questions = {r: question(r) for r in steps}
    for r in steps:
        questions[r].start()
    halos = halo_copies(0, lambda b: block_of(post, b))
    for copy in halos:
        copy.start()

    band_load.wait()
    for b in range(blocks):
        for s in range(slots):
            live = jnp.where(s < bcnt[b], 1.0, 0.0).astype(jnp.bfloat16)
            near_weights[b, pl.ds(s * tile, tile), :] = (band[b, s] * live).T
    far_load.wait()
    for r in range(peers):
        weights = far[0, mates[r]].T
        home = frow[0, mates[r]]
        for b in range(blocks):
            mine = jnp.where(home == b, 1.0, 0.0).astype(jnp.bfloat16)
            far_weights[r, :, pl.ds(b * tile, tile)] = weights * mine
    for load in loads:
        load.wait()

    wanted = {}
    for r in steps:
        questions[r].wait()
        wanted[r] = jnp.max(asked[r])
    aff_load.wait()

    cuts = [(c, min(256, classes - c)) for c in range(0, classes, 256)]
    for sweep in range(SWEEPS):
        for r in steps:
            stage[sweep, r] = own[sweep][wanted[r]]
        moves = {r: far_copy(sweep, r) for r in steps}
        for r in steps:
            moves[r].start()
        if sweep > 0:
            halos = halo_copies(sweep, lambda b: own[sweep].at[b])
            for copy in halos:
                copy.start()
        for c, w in cuts:
            acc[pl.ds(c, w), :] = jnp.dot(
                own[sweep][fblk[0, me], pl.ds(c, w), :], far_weights[0],
                preferred_element_type=jnp.float32,
            )
        for copy in halos:
            copy.wait()
        for b in range(blocks):
            lanes = pl.ds(b * tile, tile)
            for c, w in cuts:
                near = jnp.concatenate(
                    [exts[sweep][b + 1 + boff[b, s], pl.ds(c, w), :] for s in range(slots)], axis=1
                )
                acc[pl.ds(c, w), lanes] += jnp.dot(
                    near, near_weights[b], preferred_element_type=jnp.float32
                )
        for at, r in enumerate(steps):
            moves[r].wait()
            if at < len(steps) - 1:
                for c, w in cuts:
                    acc[pl.ds(c, w), :] += jnp.dot(
                        arrived[sweep, r, pl.ds(c, w), :], far_weights[r],
                        preferred_element_type=jnp.float32,
                    )
        r = steps[-1]
        squares = jnp.zeros((1, blocks * tile), jnp.float32)
        for c, w in cuts:
            mixed = acc[pl.ds(c, w), :] + jnp.dot(
                arrived[sweep, r, pl.ds(c, w), :], far_weights[r],
                preferred_element_type=jnp.float32,
            )
            mixed = propagation_weight * mixed + aff[pl.ds(c, w), :].astype(jnp.float32)
            acc[pl.ds(c, w), :] = mixed
            squares += jnp.sum(mixed * mixed, axis=0, keepdims=True)
        scale = lax.rsqrt(squares / classes + epsilon)
        for c, w in cuts:
            value = (acc[pl.ds(c, w), :] * scale).astype(jnp.bfloat16)
            if sweep < SWEEPS - 1:
                for b in range(blocks):
                    part = value[:, b * tile : (b + 1) * tile]
                    own[sweep + 1][b, pl.ds(c, w), :] = part
                    exts[sweep + 1][1 + b, pl.ds(c, w), :] = part
            else:
                out[pl.ds(c, w), :] = value


def local(peers, ring, posterior, affinity, band_tiles, offset, count, far_tiles, far_row, far_block):
    rows, classes = posterior.shape
    blocks, slots, tile, _ = band_tiles.shape
    anywhere = pl.BlockSpec(memory_space=pl.ANY)
    scalars = pl.BlockSpec(memory_space=pltpu.SMEM)
    kind = jnp.bfloat16
    result = pl.pallas_call(
        functools.partial(kernel, peers, ring),
        out_shape=jax.ShapeDtypeStruct((classes, rows), kind),
        in_specs=[anywhere] * 4 + [scalars] * 4,
        out_specs=pl.BlockSpec(memory_space=pltpu.VMEM),
        scratch_shapes=[
            [pltpu.VMEM((blocks, classes, tile), kind)] * SWEEPS,
            [pltpu.VMEM((blocks + 2, classes, tile), kind)] * SWEEPS,
            pltpu.VMEM((SWEEPS, peers, classes, tile), kind),
            pltpu.VMEM((SWEEPS, peers, classes, tile), kind),
            pltpu.VMEM((peers, 8, 128), jnp.int32),
            pltpu.VMEM((peers, 8, 128), jnp.int32),
            pltpu.VMEM((classes, rows), kind),
            pltpu.VMEM(band_tiles.shape, kind),
            pltpu.VMEM(far_tiles.shape, kind),
            pltpu.VMEM((blocks, slots * tile, tile), kind),
            pltpu.VMEM((peers, tile, rows), kind),
            pltpu.VMEM((classes, rows), jnp.float32),
            pltpu.SemaphoreType.DMA((3 + 2 * blocks,)),
            pltpu.SemaphoreType.DMA((SWEEPS, 2)),
            pltpu.SemaphoreType.DMA((SWEEPS, 2)),
            pltpu.SemaphoreType.DMA((SWEEPS, peers)),
            pltpu.SemaphoreType.DMA((SWEEPS, peers)),
            pltpu.SemaphoreType.DMA((peers,)),
            pltpu.SemaphoreType.DMA((peers,)),
        ],
        compiler_params=pltpu.CompilerParams(collective_id=0, has_side_effects=True, vmem_limit_bytes=60 * 2**20),
    )(
        posterior.T, affinity.T, band_tiles, far_tiles,
        offset, count, far_row, far_block,
    )
    return result.T


def solution(mesh):
    spread = ("gx", "gy")
    in_specs = (
        P(spread, None), P(spread, None), P(spread, None, None, None), P(spread, None),
        P(spread), P(spread, None, None, None), P(spread, None), P(spread, None),
    )

    def run(posterior, affinity, band_tiles, offset, count, far_tiles, far_row, far_block):
        return local(
            mesh.shape["gx"], mesh.shape["gy"],
            posterior, affinity, band_tiles, offset, count, far_tiles, far_row, far_block,
        )

    return jax.shard_map(run, mesh=mesh, in_specs=in_specs, out_specs=P(spread, None), check_vma=False)
```

time: 57.3 us -> 36.8 us (0.64); the launches traced: 56.3 us -> 36.6 us
  Pallas kernels: 0 us -> 34.8 us
  starting transfers between devices: 20.8 us -> 0 us
  waiting for transfers between devices: 13.7 us -> 0 us
  local copies, waits for them, and re-layouts: 15.1 us -> 1.86 us
  matrix products: 4.58 us -> 0 us
  other arithmetic: 1.81 us -> 0 us
    pallas_call x0 -> x1, Pallas kernels: none -> 34.8 us  [local(): pl.pallas_call(functools.partial(kernel, peers, ring), out_shape=jax.Shap...]
    all_to_all x3 -> x0, starting transfers between devices: 12.6 us -> none  [the longest x2 8.47 us: local(): lax.all_to_all(outgoing, 'gx', split_axis=0, concat_axis=0, tiled=True)]
    ppermute x4 -> x0, starting transfers between devices: 8.22 us -> none  [the longest x2 7.62 us: padded(): after = lax.ppermute(initial, axis, down)]
    all_to_all x3 -> x0, waiting for transfers between devices: 7.89 us -> none  [the longest x2 5.12 us: local(): lax.all_to_all(outgoing, 'gx', split_axis=0, concat_axis=0, tiled=True)]
    ppermute x4 -> x0, waiting for transfers between devices: 5.8 us -> none  [the longest x2 5.79 us: padded(): before = lax.ppermute(last, axis, up)]
    gather x4 -> x0, local copies, waits for them, and re-layouts: 5.21 us -> none  [the longest x2 3.32 us: local(): current.reshape(block_count, tile_size, class_count)[wanted]]
    dot_general x4 -> x0, matrix products: 4.58 us -> none  [the longest x2 3.44 us: local(): jnp.einsum('bsij,bsjc->bic', masked_tiles, gathered, preferred_element_ty...]
    all_to_all x3 -> x0, local copies, waits for them, and re-layouts: 4.39 us -> none  [the longest x2 3.07 us: local(): lax.all_to_all(outgoing, 'gx', split_axis=0, concat_axis=0, tiled=True)]
  transfers between devices with their start and end apart: 7 -> 0, of which waited for: 4 -> 0; matrix products, arithmetic and copies ran while one was open for 24% -> 0% of each run, Pallas kernels for 0% -> 0%
where the time goes in v1:
time: 36.8 us; the launch traced here: 36.6 us
  Pallas kernels  34.8 us (95%)
  local copies, waits for them, and re-layouts  1.86 us (5%)
    pallas_call x1, Pallas kernels, local(): pl.pallas_call(functools.partial(kernel, peers, ring), out_shape=jax.Shap...  34.8 us
    unnamed x1, local copies, waits for them, and re-layouts  1.86 us

profile of v1, /device:TPU:0, one launch (start us, length us, event | category | flops | bytes accessed | tf_op | source)
XLA Modules:
  0.0 36.6 jit_solution(7632101754303343238)
XLA Ops:
  0.0 34.8 %shard_map.82 = bf16[1000,256]{1,0:T(8,128)(2,1)} custom-call(bf16[1000,256]{1,0:T(8,128)(2,1)} %bitcast.4, bf16[1000,256]{1,0:T(8,128)(2,1)} %bitcast.5, bf16[2,4,128,128]{3,2,1,0:T(8,128)(2,1)} %band_hbm.1, bf16[1,4,128,128]{3,2,1,0:T(8,128)(2,1)} %far_hbm.1, s32[2,4]{1,0:T(2,128)} %boff.1, s32[2]{0:T(128)} %bcnt.1, s32[1,4]{1,0:T(1,128)} %frow.1, s32[1,4]{1,0:T(1,128)} %fblk.1), custom_call_target="tpu_custom_call" | custom-call | tf_op jit(solution)/shard_map/pallas_call | solution.py:184
  34.8 1.9 %copy.10 = bf16[256,1000]{0,1:T(8,128)(2,1)} copy(bf16[256,1000]{0,1:T(8,128)(2,1)} %bitcast.3) | data formatting | bytes 1024000

commit v2 on v0

v2 whole, which is shorter than its diff:
```python
import functools

import jax
import jax.numpy as jnp
from jax import lax
from jax.experimental import pallas as pl
from jax.experimental.pallas import tpu as pltpu
from jax.sharding import PartitionSpec as P

SWEEPS = 2
propagation_weight = 0.9
epsilon = 1e-06
FIRST = 128
PIECES = 3
BRIDGE = 1
MESH = pl.DeviceIdType.MESH


def partner(me, step, peers):
    total = 0
    bit = 1
    while bit < peers:
        here = lax.rem(me // bit, 2)
        total = total + bit * (lax.rem(here + 1, 2) if step & bit else here)
        bit *= 2
    return total


def chunks_of(classes):
    first = min(FIRST, classes)
    cuts = [(0, first)]
    rest = classes - first
    if rest:
        size = -(-rest // (PIECES * 16)) * 16
        cuts += [(c, min(size, classes - c)) for c in range(first, classes, size)]
    return cuts


def kernel(
    peers, ring, cuts,
    post, aff_hbm, band_hbm, far_hbm, boff_hbm, bcnt_hbm, frow_hbm, fblk_hbm,
    out, scale_out,
    own, exts, early, stage, arrived, ask, asked, aff, band, far, near_weights, far_weights, acc,
    boff, bcnt, frow, fblk, scales, far_scale_out, far_scale_in,
    load_sem, halo_send, halo_recv, far_send, far_recv, ask_send, ask_recv, scale_send, scale_recv,
):
    me = lax.axis_index("gx")
    spot = lax.axis_index("gy")
    up = lax.rem(spot + 1, ring)
    down = lax.rem(spot + ring - 1, ring)
    blocks, slots, tile, _ = band.shape
    classes = post.shape[0]
    steps = sorted(range(1, peers), key=lambda r: (-bin(r).count("1"), r))
    mates = {r: partner(me, r, peers) for r in range(peers)}

    barrier = pltpu.get_barrier_semaphore()
    for side in (up, down):
        pl.semaphore_signal(barrier, inc=1, device_id={"gy": side}, device_id_type=MESH)
    for r in steps:
        pl.semaphore_signal(barrier, inc=1, device_id={"gx": mates[r]}, device_id_type=MESH)

    pending = []

    def load(source, target):
        copy = pltpu.make_async_copy(source, target, load_sem.at[len(pending)])
        copy.start()
        pending.append(copy)
        return copy

    words = [
        load(source, target)
        for source, target in ((fblk_hbm, fblk), (frow_hbm, frow), (bcnt_hbm, bcnt), (boff_hbm, boff))
    ]
    mine = [load(post.at[:, pl.ds(b * tile, tile)], own[0].at[b]) for b in range(blocks)]
    band_load = load(band_hbm, band)
    far_load = load(far_hbm, far)
    aff_load = load(aff_hbm, aff)
    for copy in words:
        copy.wait()
    for r in steps:
        ask[r] = jnp.full(ask.shape[1:], fblk[0, mates[r]], jnp.int32)
    for copy in mine:
        copy.wait()
    for k, (c, w) in enumerate(cuts):
        for b in range(blocks):
            exts[0][k][1 + b] = own[0][b, pl.ds(c, w), :]
    pl.semaphore_wait(barrier, len(steps) + 2)

    def to_mate(r, source, target, send, recv):
        return pltpu.make_async_remote_copy(
            src_ref=source, dst_ref=target, send_sem=send, recv_sem=recv,
            device_id={"gx": mates[r]}, device_id_type=MESH,
        )

    def to_sides(first, last, before, after, send, recv):
        return [
            pltpu.make_async_remote_copy(
                src_ref=source, dst_ref=target, send_sem=send.at[i], recv_sem=recv.at[i],
                device_id={"gy": side}, device_id_type=MESH,
            )
            for i, (source, target, side) in enumerate(((last, before, up), (first, after, down)))
        ]

    def send_halo(sweep, k):
        c, w = cuts[k]
        copies = to_sides(
            own[sweep].at[0, pl.ds(c, w)], own[sweep].at[blocks - 1, pl.ds(c, w)],
            exts[sweep][k].at[0], exts[sweep][k].at[blocks + 1],
            halo_send.at[sweep, k], halo_recv.at[sweep, k],
        )
        for copy in copies:
            copy.start()
        return copies

    def send_far(sweep, k):
        c, w = cuts[k]
        for r in steps:
            stage[sweep, r, pl.ds(c, w), :] = own[sweep][wanted[r], pl.ds(c, w), :]
        copies = [
            to_mate(
                r, stage.at[sweep, r, pl.ds(c, w)], arrived.at[sweep, r, pl.ds(c, w)],
                far_send.at[sweep, k, r], far_recv.at[sweep, k, r],
            )
            for r in steps
        ]
        for copy in copies:
            copy.start()
        return copies

    questions = {r: to_mate(r, ask.at[r], asked.at[r], ask_send.at[r], ask_recv.at[r]) for r in steps}
    for r in steps:
        questions[r].start()
    c, w = cuts[0]
    far_moves, halo_moves = {}, {}
    far_moves[0, 0] = [
        to_mate(
            r, own[0].at[:, pl.ds(c, w)], early.at[r], far_send.at[0, 0, r], far_recv.at[0, 0, r]
        )
        for r in steps
    ]
    for copy in far_moves[0, 0]:
        copy.start()
    for k in range(len(cuts)):
        halo_moves[0, k] = send_halo(0, k)

    wanted = {}
    for r in steps:
        questions[r].wait()
        wanted[r] = jnp.max(asked[r])
    for k in range(1, len(cuts)):
        far_moves[0, k] = send_far(0, k)

    def weights():
        for b in range(blocks):
            for s in range(slots):
                live = jnp.where(s < bcnt[b], 1.0, 0.0)
                part = band[b, s].astype(jnp.float32) * live
                near_weights[b, pl.ds(s * tile, tile), :] = part.astype(jnp.bfloat16).T
        for r in range(peers):
            part = far[0, mates[r]].T
            home = frow[0, mates[r]]
            for b in range(blocks):
                chosen = jnp.where(home == b, 1.0, 0.0).astype(jnp.bfloat16)
                far_weights[pl.ds(r * tile, tile), pl.ds(b * tile, tile)] = part * chosen

    band_load.wait()
    far_load.wait()
    weights()
    aff_load.wait()

    def times(value, row):
        return (value.astype(jnp.float32) * row[0:1, :]).astype(jnp.bfloat16)

    def keep(sweep, k, value):
        c, w = cuts[k]
        for b in range(blocks):
            part = value[:, b * tile : (b + 1) * tile]
            own[sweep][b, pl.ds(c, w), :] = part
            exts[sweep][k][1 + b] = part

    scale_moves = {}
    for sweep in range(SWEEPS):
        squares = jnp.zeros((1, blocks * tile), jnp.float32)
        for k, (c, w) in enumerate(cuts):
            rows = pl.ds(c, w)
            raw = sweep > 0 and k < BRIDGE
            if raw and k == 0:
                for copy in scale_moves[sweep]:
                    copy.wait()
            for copy in halo_moves[sweep, k]:
                copy.wait_recv() if raw else copy.wait()
            if raw:
                for e in (0, blocks + 1):
                    exts[sweep][k][e] = times(exts[sweep][k][e], scales[e])
            near = [
                jnp.dot(
                    jnp.concatenate(
                        [exts[sweep][k][b + 1 + boff[b, s]] for s in range(slots)], axis=1
                    ),
                    near_weights[b], preferred_element_type=jnp.float32,
                )
                for b in range(blocks)
            ]
            for copy in far_moves[sweep, k]:
                copy.wait()
            parts = [own[sweep][fblk[0, me], rows, :]]
            for r in range(1, peers):
                if sweep == 0 and k == 0:
                    parts.append(early[r, fblk[0, mates[r]]])
                elif raw:
                    parts.append(times(arrived[sweep, r, rows, :], far_scale_in[r]))
                else:
                    parts.append(arrived[sweep, r, rows, :])
            mixed = jnp.dot(
                jnp.concatenate(parts, axis=1), far_weights[...],
                preferred_element_type=jnp.float32,
            )
            mixed = mixed + jnp.concatenate(near, axis=1)
            mixed = propagation_weight * mixed + aff[rows, :].astype(jnp.float32)
            squares += jnp.sum(mixed * mixed, axis=0, keepdims=True)
            if sweep < SWEEPS - 1:
                acc[rows, :] = mixed
                if k < BRIDGE:
                    keep(sweep + 1, k, mixed.astype(jnp.bfloat16))
                    far_moves[sweep + 1, k] = send_far(sweep + 1, k)
                    halo_moves[sweep + 1, k] = send_halo(sweep + 1, k)
            else:
                out[rows, :] = mixed
        scale = lax.rsqrt(squares / classes + epsilon)
        if sweep == SWEEPS - 1:
            scale_out[...] = jnp.broadcast_to(scale, scale_out.shape)
            continue
        for b in range(blocks):
            scales[1 + b] = jnp.broadcast_to(scale[:, b * tile : (b + 1) * tile], (8, tile))
        for r in steps:
            row = scales[1]
            for b in range(1, blocks):
                row = jnp.where(wanted[r] == b, scales[1 + b], row)
            far_scale_out[r] = row
        scale_moves[sweep + 1] = [
            to_mate(r, far_scale_out.at[r], far_scale_in.at[r], scale_send.at[r], scale_recv.at[r])
            for r in steps
        ] + to_sides(
            scales.at[1], scales.at[blocks], scales.at[0], scales.at[blocks + 1],
            scale_send.at[pl.ds(peers, 2)], scale_recv.at[pl.ds(peers, 2)],
        )
        for copy in scale_moves[sweep + 1]:
            copy.start()
        for k, (c, w) in enumerate(cuts):
            value = (acc[pl.ds(c, w), :] * scale).astype(jnp.bfloat16)
            if k >= BRIDGE:
                keep(sweep + 1, k, value)
                far_moves[sweep + 1, k] = send_far(sweep + 1, k)
                halo_moves[sweep + 1, k] = send_halo(sweep + 1, k)
        for k, (c, w) in enumerate(cuts[:BRIDGE]):
            value = (acc[pl.ds(c, w), :] * scale).astype(jnp.bfloat16)
            for copy in halo_moves[sweep + 1, k]:
                copy.wait_send()
            keep(sweep + 1, k, value)


def local(peers, ring, posterior, affinity, band_tiles, offset, count, far_tiles, far_row, far_block):
    rows, classes = posterior.shape
    blocks, slots, tile, _ = band_tiles.shape
    stored = pl.BlockSpec(memory_space=pltpu.HBM)
    kind = jnp.bfloat16
    cuts = chunks_of(classes)
    pieces = len(cuts)
    scratch = [
        [pltpu.VMEM((blocks, classes, tile), kind)] * SWEEPS,
        [[pltpu.VMEM((blocks + 2, w, tile), kind) for _, w in cuts] for _ in range(SWEEPS)],
        pltpu.VMEM((peers, blocks, cuts[0][1], tile), kind),
        pltpu.VMEM((SWEEPS, peers, classes, tile), kind),
        pltpu.VMEM((SWEEPS, peers, classes, tile), kind),
        pltpu.VMEM((peers, 8, 128), jnp.int32),
        pltpu.VMEM((peers, 8, 128), jnp.int32),
        pltpu.VMEM((classes, rows), kind),
        pltpu.VMEM(band_tiles.shape, kind),
        pltpu.VMEM(far_tiles.shape, kind),
        pltpu.VMEM((blocks, slots * tile, tile), kind),
        pltpu.VMEM((peers * tile, rows), kind),
        pltpu.VMEM((classes, rows), jnp.float32),
        pltpu.SMEM(offset.shape, jnp.int32),
        pltpu.SMEM(count.shape, jnp.int32),
        pltpu.SMEM(far_row.shape, jnp.int32),
        pltpu.SMEM(far_block.shape, jnp.int32),
        pltpu.VMEM((blocks + 2, 8, tile), jnp.float32),
        pltpu.VMEM((peers, 8, tile), jnp.float32),
        pltpu.VMEM((peers, 8, tile), jnp.float32),
        pltpu.SemaphoreType.DMA((7 + blocks,)),
        pltpu.SemaphoreType.DMA((SWEEPS, pieces, 2)),
        pltpu.SemaphoreType.DMA((SWEEPS, pieces, 2)),
        pltpu.SemaphoreType.DMA((SWEEPS, pieces, peers)),
        pltpu.SemaphoreType.DMA((SWEEPS, pieces, peers)),
        pltpu.SemaphoreType.DMA((peers,)),
        pltpu.SemaphoreType.DMA((peers,)),
        pltpu.SemaphoreType.DMA((peers + 2,)),
        pltpu.SemaphoreType.DMA((peers + 2,)),
    ]
    mixed, scale = pl.pallas_call(
        functools.partial(kernel, peers, ring, cuts),
        out_shape=(
            jax.ShapeDtypeStruct((classes, rows), jnp.float32),
            jax.ShapeDtypeStruct((8, rows), jnp.float32),
        ),
        in_specs=[stored] * 8,
        out_specs=(pl.BlockSpec(memory_space=pltpu.VMEM),) * 2,
        scratch_shapes=scratch,
        compiler_params=pltpu.CompilerParams(
            collective_id=0, has_side_effects=True, vmem_limit_bytes=60 * 2**20
        ),
    )(
        posterior.T, affinity.T, band_tiles, far_tiles,
        offset, count, far_row, far_block,
    )
    return (mixed * scale[0:1, :]).astype(kind).T


def solution(mesh):
    spread = ("gx", "gy")
    in_specs = (
        P(spread, None), P(spread, None), P(spread, None, None, None), P(spread, None),
        P(spread), P(spread, None, None, None), P(spread, None), P(spread, None),
    )

    def run(posterior, affinity, band_tiles, offset, count, far_tiles, far_row, far_block):
        return local(
            mesh.shape["gx"], mesh.shape["gy"],
            posterior, affinity, band_tiles, offset, count, far_tiles, far_row, far_block,
        )

    return jax.shard_map(run, mesh=mesh, in_specs=in_specs, out_specs=P(spread, None), check_vma=False)
```

time: 57.3 us -> 35.4 us (0.62); the launches traced: 56.3 us -> 35.2 us
  Pallas kernels: 0 us -> 32.4 us
  starting transfers between devices: 20.8 us -> 0 us
  local copies, waits for them, and re-layouts: 15.1 us -> 0.7 us
  waiting for transfers between devices: 13.7 us -> 0 us
  matrix products: 4.58 us -> 0 us
    pallas_call x0 -> x1, Pallas kernels: none -> 32.4 us  [local(): pl.pallas_call(functools.partial(kernel, peers, ring, cuts), out_shape=(j...]
    all_to_all x3 -> x0, starting transfers between devices: 12.6 us -> none  [the longest x2 8.47 us: local(): lax.all_to_all(outgoing, 'gx', split_axis=0, concat_axis=0, tiled=True)]
    ppermute x4 -> x0, starting transfers between devices: 8.22 us -> none  [the longest x2 7.62 us: padded(): after = lax.ppermute(initial, axis, down)]
    all_to_all x3 -> x0, waiting for transfers between devices: 7.89 us -> none  [the longest x2 5.12 us: local(): lax.all_to_all(outgoing, 'gx', split_axis=0, concat_axis=0, tiled=True)]
    ppermute x4 -> x0, waiting for transfers between devices: 5.8 us -> none  [the longest x2 5.79 us: padded(): before = lax.ppermute(last, axis, up)]
    gather x4 -> x0, local copies, waits for them, and re-layouts: 5.21 us -> none  [the longest x2 3.32 us: local(): current.reshape(block_count, tile_size, class_count)[wanted]]
    dot_general x4 -> x0, matrix products: 4.58 us -> none  [the longest x2 3.44 us: local(): jnp.einsum('bsij,bsjc->bic', masked_tiles, gathered, preferred_element_ty...]
    all_to_all x3 -> x0, local copies, waits for them, and re-layouts: 4.39 us -> none  [the longest x2 3.07 us: local(): lax.all_to_all(outgoing, 'gx', split_axis=0, concat_axis=0, tiled=True)]
  transfers between devices with their start and end apart: 7 -> 0, of which waited for: 4 -> 0; matrix products, arithmetic and copies ran while one was open for 24% -> 0% of each run, Pallas kernels for 0% -> 0%
where the time goes in v2:
time: 35.4 us; the launch traced here: 35.2 us
  Pallas kernels  32.4 us (92%)
  other arithmetic  2.08 us (6%)
  local copies, waits for them, and re-layouts  0.7 us (2%)
    pallas_call x1, Pallas kernels, local(): pl.pallas_call(functools.partial(kernel, peers, ring, cuts), out_shape=(j...  32.4 us
    transpose x1, other arithmetic, local(): return (mixed * scale[0:1, :]).astype(kind).T  2.08 us

profile of v2, /device:TPU:0, one launch (start us, length us, event | category | flops | bytes accessed | tf_op | source)
XLA Modules:
  0.0 35.2 jit_solution(10811267503442797160)
XLA Ops:
  0.0 32.4 %shard_map.82 = (f32[1000,256]{1,0:T(8,128)}, f32[8,256]{1,0:T(8,128)}) custom-call(bf16[1000,256]{1,0:T(8,128)(2,1)} %bitcast.5, bf16[1000,256]{1,0:T(8,128)(2,1)} %bitcast.6, bf16[2,4,128,128]{3,2,1,0:T(8,128)(2,1)} %band_hbm.1, bf16[1,4,128,128]{3,2,1,0:T(8,128)(2,1)} %far_hbm.1, s32[2,4]{1,0:T(2,128)} %boff_hbm.1, s32[2]{0:T(128)} %bcnt_hbm.1, ...), custom_call_target="tpu_custom_call" | custom-call | tf_op jit(solution)/shard_map/pallas_call | solution.py:300
  32.4 0.7 %slice.3 = f32[1,256]{1,0:T(1,128)S(1)} slice(f32[8,256]{1,0:T(8,128)} %get-tuple-element.8), slice={[0:1], [0:256]} | slice | bytes 2048 | tf_op jit(solution)/shard_map/slice | solution.py:316
  33.1 2.1 %fusion = bf16[256,1000]{0,1:T(8,128)(2,1)} fusion(f32[1000,256]{1,0:T(8,128)} %get-tuple-element.7, f32[256]{0:T(256)S(1)} %bitcast.7), kind=kLoop, calls=%fused_computation.1 | loop fusion | flops 512000 | bytes 1537024 | tf_op jit(solution)/shard_map/transpose | solution.py:316

commit v3 on v2

--- a/solution.py
+++ b/solution.py
@@ -39,7 +39,7 @@
 def kernel(
     peers, ring, cuts,
     post, aff_hbm, band_hbm, far_hbm, boff_hbm, bcnt_hbm, frow_hbm, fblk_hbm,
-    out, scale_out,
+    out,
     own, exts, early, stage, arrived, ask, asked, aff, band, far, near_weights, far_weights, acc,
     boff, bcnt, frow, fblk, scales, far_scale_out, far_scale_in,
     load_sem, halo_send, halo_recv, far_send, far_recv, ask_send, ask_recv, scale_send, scale_recv,
@@ -225,10 +225,11 @@
                     far_moves[sweep + 1, k] = send_far(sweep + 1, k)
                     halo_moves[sweep + 1, k] = send_halo(sweep + 1, k)
             else:
-                out[rows, :] = mixed
+                acc[rows, :] = mixed
         scale = lax.rsqrt(squares / classes + epsilon)
         if sweep == SWEEPS - 1:
-            scale_out[...] = jnp.broadcast_to(scale, scale_out.shape)
+            for c, w in cuts:
+                out[pl.ds(c, w), :] = (acc[pl.ds(c, w), :] * scale).astype(jnp.bfloat16)
             continue
         for b in range(blocks):
             scales[1 + b] = jnp.broadcast_to(scale[:, b * tile : (b + 1) * tile], (8, tile))
@@ -297,23 +298,25 @@
         pltpu.SemaphoreType.DMA((peers + 2,)),
         pltpu.SemaphoreType.DMA((peers + 2,)),
     ]
-    mixed, scale = pl.pallas_call(
+    held = min(8 * rows * classes * (3 + 2 * peers) + 20 * 2**20, 60 * 2**20)
+    result = pl.pallas_call(
         functools.partial(kernel, peers, ring, cuts),
-        out_shape=(
-            jax.ShapeDtypeStruct((classes, rows), jnp.float32),
-            jax.ShapeDtypeStruct((8, rows), jnp.float32),
-        ),
+        out_shape=jax.ShapeDtypeStruct((classes, rows), kind),
         in_specs=[stored] * 8,
-        out_specs=(pl.BlockSpec(memory_space=pltpu.VMEM),) * 2,
+        out_specs=pl.BlockSpec(memory_space=pltpu.VMEM),
         scratch_shapes=scratch,
         compiler_params=pltpu.CompilerParams(
-            collective_id=0, has_side_effects=True, vmem_limit_bytes=60 * 2**20
+            collective_id=0, has_side_effects=True, vmem_limit_bytes=held
         ),
     )(
-        posterior.T, affinity.T, band_tiles, far_tiles,
-        offset, count, far_row, far_block,
+        *[
+            pltpu.with_memory_space_constraint(value, pltpu.HBM)
+            for value in (
+                posterior.T, affinity.T, band_tiles, far_tiles, offset, count, far_row, far_block
+            )
+        ]
     )
-    return (mixed * scale[0:1, :]).astype(kind).T
+    return result.T
 
 
 def solution(mesh):

time: 35.4 us -> 32.5 us (0.918)
  other arithmetic: 2.08 us -> 0 us
  Pallas kernels: 32.4 us -> 31.5 us
    transpose x1 -> x0, other arithmetic: 2.08 us -> none  [local(): return (mixed * scale[0:1, :]).astype(kind).T]
    pallas_call x1, Pallas kernels: 32.4 us -> 31.5 us  [local(): pl.pallas_call(functools.partial(kernel, peers, ring, cuts), out_shape=ja...]
    unnamed x0 -> x1, local copies, waits for them, and re-layouts: none -> 0.79 us
    slice x1 -> x0, local copies, waits for them, and re-layouts: 0.7 us -> none  [local(): return (mixed * scale[0:1, :]).astype(kind).T]
where the time goes in v3:
time: 32.5 us; the launch traced here: 32.3 us
  Pallas kernels  31.5 us (97%)
  local copies, waits for them, and re-layouts  0.79 us (2%)
    pallas_call x1, Pallas kernels, local(): pl.pallas_call(functools.partial(kernel, peers, ring, cuts), out_shape=ja...  31.5 us
    unnamed x1, local copies, waits for them, and re-layouts  0.79 us

profile of v3, /device:TPU:0, one launch (start us, length us, event | category | flops | bytes accessed | tf_op | source)
XLA Modules:
  0.0 32.3 jit_solution(7196632838494975519)
XLA Ops:
  0.0 31.5 %shard_map.82 = bf16[1000,256]{1,0:T(8,128)(2,1)S(1)} custom-call(bf16[1000,256]{1,0:T(8,128)(2,1)} %bitcast.4, bf16[1000,256]{1,0:T(8,128)(2,1)} %bitcast.5, bf16[2,4,128,128]{3,2,1,0:T(8,128)(2,1)} %band_hbm.1, bf16[1,4,128,128]{3,2,1,0:T(8,128)(2,1)} %far_hbm.1, s32[2,4]{1,0:T(2,128)} %boff_hbm.1, s32[2]{0:T(128)} %bcnt_hbm.1, s32[1,4]{1,0:T(1,128)} %frow_hbm.1, ...), custom_call_target="tpu_custom_call" | custom-call | tf_op jit(solution)/shard_map/pallas_call | solution.py:302
  31.5 0.8 %copy.10 = bf16[256,1000]{0,1:T(8,128)(2,1)} copy(bf16[256,1000]{0,1:T(8,128)(2,1)S(1)} %bitcast.3) | data formatting | bytes 1024000
